TPU v7x, 512 devices: a whole 4x8x8 slice. The times are simulated.
512 devices in a mesh: dp: 64 (over z, y_hi, core), stat: 8 (over x, y_lo).
Axes of the slice: x: 4, y: 8 (y_hi: 4, y_lo: 2; y = y_hi * 2 + y_lo), z: 8, core: 2. Of those that a mesh axis runs over, the one named last changes fastest.
Arguments:
- activations: bfloat16 [65536, 8192], P('dp'), may hold values from -16 to 16
- out_grads: bfloat16 [65536, 1024], P('dp', 'stat'), may hold values from -0.0234375 to 0.0234375
- stat_old: float32 [192, 128, 128], P('dp'), may hold values from -0.24 to 0.24
- pattern: int32 [192, 2], replicated, may hold values from 0 to 63, as said below
- holders: int32 [192], replicated, may hold values from 0 to 63, as said below
Outputs:
- direction: float32 [8192, 1024], P('dp', 'stat')
- statistics: float32 [192, 128, 128], P('dp', 'stat')
Inputs may be any that keep to these rules, and one draw needn't show every extreme that they name: `pattern`: every diagonal pair (a, a) for a in 0 to 63 appears exactly once; every other entry has different row and column blocks; half of those are band pairs (column block next to the row block, cyclically), the rest reach anywhere. `holders`: every dp index holds exactly 3 entries; the diagonal entry (a, a) is held by the dp index whose weight rows contain row a * 128.
All inputs are finite; a program needn't handle non-finite values.
Results may differ from a plain program's by a relative error of at most 0.003.
Values may be sent and summed in bfloat16 or wider, within the bound.
No kernel may reach another device: no remote copies, remote signals or barrier semaphores. Data moves between devices by JAX's collectives and lax.ppermute only.
A program may use at most 192 MiB of HBM per device.

v0:
```python
import jax
import jax.numpy as jnp
from jax import lax
from jax.sharding import PartitionSpec as P

ITERS = 5
beta_stat = 0.6
damping = 0.75


def inverse_root(matrix):
    size = matrix.shape[0]
    eye = jnp.eye(size, dtype=matrix.dtype)
    sym = 0.5 * (matrix + matrix.T) + damping * eye
    scale = jnp.sqrt(jnp.sum(sym * sym))
    current = sym / scale
    result = eye
    for sweep in range(ITERS):
        factor = (5.0 * eye - current) * 0.25
        result = jnp.dot(result, factor, precision=lax.Precision.HIGHEST)
        square = jnp.dot(factor, factor, precision=lax.Precision.HIGHEST)
        fourth = jnp.dot(square, square, precision=lax.Precision.HIGHEST)
        current = jnp.dot(fourth, current, precision=lax.Precision.HIGHEST)
    return result * scale ** (-0.25)


def per_device(activations, out_grads, stat_old, pattern, holders):
    position = lax.axis_index("dp")
    stat_pos = lax.axis_index("stat")
    stat_count = lax.axis_size("stat")
    group_count = lax.axis_size("dp")
    block = stat_old.shape[2]
    held = stat_old.shape[0]
    width_cols = out_grads.shape[1]
    total_cols = width_cols * stat_count
    own_rows = activations.shape[1] // group_count
    own_panels = own_rows // block
    share_rows = block // stat_count
    partial_value = lax.dot_general(
        activations, out_grads, (((0,), (0,)), ((), ())), preferred_element_type=jnp.float32
    )
    grad_own = lax.psum_scatter(partial_value, "dp", scatter_dimension=0, tiled=True)
    grad_b = grad_own.astype(jnp.bfloat16)
    grad_full = lax.all_gather(grad_b, "dp", axis=0, tiled=True)
    entries = jnp.arange(holders.shape[0], dtype=jnp.int32)
    same_holder = holders[None, :] == holders[:, None]
    earlier = entries[None, :] < entries[:, None]
    within = jnp.sum((same_holder & earlier).astype(jnp.int32), axis=1)
    slot_ids = jnp.arange(held, dtype=jnp.int32)
    picked = ((holders[None, :] == position) & (within[None, :] == slot_ids[:, None])).astype(
        jnp.int32
    )
    row_blocks = jnp.sum(picked * pattern[None, :, 0], axis=1)
    col_blocks = jnp.sum(picked * pattern[None, :, 1], axis=1)

    def panel_at(index):
        return lax.dynamic_slice_in_dim(grad_full, index * block, block, 0)

    first = jax.vmap(panel_at)(row_blocks)
    second = jax.vmap(panel_at)(col_blocks)
    partial_gram = jnp.einsum("jrc,jsc->jrs", first, second, preferred_element_type=jnp.float32)
    panel_ids = position * own_panels + jnp.arange(own_panels, dtype=jnp.int32)
    select = (
        (row_blocks[None, :] == panel_ids[:, None]) & (col_blocks[None, :] == panel_ids[:, None])
    ).astype(jnp.float32)
    gram = lax.psum(partial_gram, "stat") / total_cols
    new_full = beta_stat * stat_old + (1.0 - beta_stat) * gram
    statistics = lax.dynamic_slice_in_dim(new_full, stat_pos * share_rows, share_rows, 1)
    diag_full = jnp.einsum("ij,jrs->irs", select, new_full, precision=lax.Precision.HIGHEST)
    roots = jax.vmap(inverse_root)(diag_full)
    stacked = grad_b.reshape(own_panels, block, width_cols).astype(jnp.float32)
    direction = jnp.einsum("irs,isc->irc", roots, stacked, precision=lax.Precision.HIGHEST).reshape(
        own_rows, width_cols
    )
    return (direction, statistics)


def solution(mesh):
    placed = (P("dp", None), P("dp", "stat"), P("dp", None, None), P(), P())
    return jax.shard_map(
        per_device,
        mesh=mesh,
        in_specs=placed,
        out_specs=(P("dp", "stat"), P("dp", "stat", None)),
        check_vma=False,
    )
```

profile of v0, /device:TPU:16, one launch (start us, length us, event | category | flops | bytes accessed | tf_op | source)
XLA Modules:
  0.0 372.1 jit_solution(4225835935777401481)
XLA Ops:
  7.2 0.9 copy-done
  8.1 10.1 %fusion.82 = f32[8192,128]{1,0:T(8,128)} fusion(bf16[1024,8192]{1,0:T(8,128)(2,1)} %param.5, bf16[1024,128]{1,0:T(8,128)(2,1)S(1)} %copy-done), kind=kOutput, calls=%fused_computation.101 | convolution fusion | flops 2147483648 | bytes 21233664 | tf_op jit(solution)/shard_map/dot_general | solution.py:39
  18.3 161.4 %reduce-scatter.2.cloned.1.call-done = f32[128,128]{1,0:T(8,128)} async-done(((f32[8192,128]{1,0:T(8,128)}), f32[128,128]{1,0:T(8,128)}) %reduce-scatter.2.cloned.1.call-update) | async-done | bytes 65552 | tf_op jit(solution)/shard_map/reduce_scatter | solution.py:42
  179.7 1.5 convert_element_type.5
  181.7 82.5 %all-gather.2.cloned.1.call-done = bf16[8192,128]{1,0:T(8,128)(2,1)} async-done(((bf16[128,128]{1,0:T(8,128)(2,1)}), bf16[8192,128]{1,0:T(8,128)(2,1)}) %all-gather.2.cloned.1.call-update) | async-done | bytes 2097168 | tf_op jit(solution)/shard_map/all_gather | solution.py:44
  264.2 5.7 %while.2 = (s32[]{:T(128)}, bf16[8192,128]{1,0:T(8,128)(2,1)}, s32[3,2]{0,1:T(2,128)S(1)}, bf16[3,128,128]{2,1,0:T(8,128)(2,1)S(1)}, s32[]{:T(128)}) while((s32[]{:T(128)}, bf16[8192,128]{1,0:T(8,128)(2,1)}, s32[3,2]{0,1:T(2,128)S(1)}, bf16[3,128,128]{2,1,0:T(8,128)(2,1)S(1)}, s32[]{:T(128)}) %tuple.34), condition=%wide.while_cond, body=%wide.while_body.sunk | while | flops 2 | bytes 65641 | solution.py:57
  264.3 0.5 slice.34
  264.8 1.3 bitcast_dynamic-update-slice_fusion.4
  266.2 0.5 slice.34
  266.7 1.3 bitcast_dynamic-update-slice_fusion.4
  268.2 0.5 slice.34
  268.6 1.3 bitcast_dynamic-update-slice_fusion.4
  270.0 6.1 %while.3 = (s32[]{:T(128)}, bf16[8192,128]{1,0:T(8,128)(2,1)}, s32[3,2]{0,1:T(2,128)S(1)}, bf16[3,128,128]{2,1,0:T(8,128)(2,1)S(1)}, s32[]{:T(128)}) while((s32[]{:T(128)}, bf16[8192,128]{1,0:T(8,128)(2,1)}, s32[3,2]{0,1:T(2,128)S(1)}, bf16[3,128,128]{2,1,0:T(8,128)(2,1)S(1)}, s32[]{:T(128)}) %tuple.46), condition=%wide.while_cond.1, body=%wide.while_body.1.sunk | while | flops 2 | bytes 65641 | solution.py:57
  270.1 0.5 slice.35
  270.6 1.4 bitcast_dynamic-update-slice_fusion.5
  272.1 0.5 slice.35
  272.6 1.4 bitcast_dynamic-update-slice_fusion.5
  274.2 0.5 slice.35
  274.7 1.4 bitcast_dynamic-update-slice_fusion.5
  276.1 0.9 fusion.83
  277.0 80.5 %all-reduce.4.cloned.1.call-done = f32[3,128,128]{2,1,0:T(8,128)} async-done(((f32[3,128,128]{2,1,0:T(8,128)}), f32[3,128,128]{2,1,0:T(8,128)}) %all-reduce.4.cloned.1.call-update) | async-done | bytes 196624 | tf_op jit(solution)/shard_map/psum | solution.py:66
  357.6 1.0 multiply_add_fusion
  358.5 0.5 fusion.1
  359.1 0.6 multiply_reduce_fusion
  361.3 0.2 fusion.23
  361.5 0.2 fusion.25
  362.1 0.2 fusion.19
  362.3 0.2 fusion.21
  363.0 0.2 fusion.15
  363.2 0.2 fusion.17
  364.1 0.8 fusion.90
  364.9 0.6 constant_dynamic-slice_fusion.2
  (43 shorter events, 3.4 us)
Async XLA Ops:
  7.2 1.0 copy-start
  7.2 172.6 %reduce-scatter.2.cloned.1.call-start = ((), (), s32[]{:S(2)}) async-start(), calls=%async_computation.1 | async-start | bytes 4259840 | tf_op jit(solution)/shard_map/reduce_scatter | solution.py:42
  18.2 163.1 %copy-start.3 = (s32[192]{0:T(256)S(1)}, s32[192]{0:T(256)}, u32[]{:S(2)}) copy-start(s32[192]{0:T(256)} %param.9) | copy-start | bytes 2308
  18.2 163.3 %copy-start.4 = (s32[192,2]{0,1:T(2,128)S(1)}, s32[192,2]{0,1:T(2,128)}, u32[]{:S(2)}) copy-start(s32[192,2]{0,1:T(2,128)} %param.8) | copy-start | bytes 4612
  18.2 339.4 %copy-start.2 = (f32[3,128,128]{2,1,0:T(8,128)S(1)}, f32[3,128,128]{2,1,0:T(8,128)}, u32[]{:S(2)}) copy-start(f32[3,128,128]{2,1,0:T(8,128)} %param.7) | copy-start | bytes 589828
  18.2 246.0 %all-gather.2.cloned.1.call-start = ((), (), s32[]{:S(2)}) async-start(), calls=%async_computation.2 | async-start | bytes 2129920 | tf_op jit(solution)/shard_map/all_gather | solution.py:44
  181.2 182.9 %copy-start.1 = (bf16[128,128]{1,0:T(8,128)(2,1)S(1)}, bf16[128,128]{1,0:T(8,128)(2,1)}, u32[]{:S(2)}) copy-start(bf16[128,128]{1,0:T(8,128)(2,1)} %convert_element_type.5) | copy-start | bytes 98308
  181.2 176.3 %all-reduce.4.cloned.1.call-start = ((), (), s32[]{:S(2)}) async-start(), calls=%async_computation.3 | async-start | bytes 393216 | tf_op jit(solution)/shard_map/psum | solution.py:66
Sparse Core Ops, SparseCore 0:
  18.4 161.3 reduce-scatter.1
  183.7 80.5 all-gather.1
  277.1 80.3 all-reduce.3
where the time goes:
time: 373 us; the launch traced here: 372 us
  waiting for transfers between devices  325 us (87%)
  matrix products  15.7 us (4%)
  between operations  14.8 us (4%)
  local copies, waits for them, and re-layouts  13.4 us (4%)
    reduce_scatter x1, waiting for transfers between devices, per_device(): lax.psum_scatter(partial_value, 'dp', scatter_dimension=0, tiled=True)  161 us
    all_gather x1, waiting for transfers between devices, per_device(): grad_full = lax.all_gather(grad_b, 'dp', axis=0, tiled=True)  82.5 us
    psum x1, waiting for transfers between devices, per_device(): gram = lax.psum(partial_gram, 'stat') / total_cols  80.5 us
    gather x18, local copies, waits for them, and re-layouts  11.7 us
    dot_general x1, matrix products, per_device(): lax.dot_general(activations, out_grads, (((0,), (0,)), ((), ())), preferr...  10.1 us
  transfers between devices with their start and end apart: 3, of which 3 were waited for; matrix products, arithmetic and copies ran while one was open for 0% of the time, Pallas kernels for 0%

commit v1 on v0

--- a/solution.py
+++ b/solution.py
@@ -2,6 +2,7 @@
 import jax.numpy as jnp
 from jax import lax
 from jax.sharding import PartitionSpec as P
+from jax.lax import all_gather
 
 ITERS = 5
 beta_stat = 0.6
@@ -63,7 +64,8 @@
     select = (
         (row_blocks[None, :] == panel_ids[:, None]) & (col_blocks[None, :] == panel_ids[:, None])
     ).astype(jnp.float32)
-    gram = lax.psum(partial_gram, "stat") / total_cols
+    serve_kinds_on_mesh = lambda inner_x: all_gather(inner_x, "stat").sum(axis=0)
+    gram = serve_kinds_on_mesh(partial_gram) / total_cols
     new_full = beta_stat * stat_old + (1.0 - beta_stat) * gram
     statistics = lax.dynamic_slice_in_dim(new_full, stat_pos * share_rows, share_rows, 1)
     diag_full = jnp.einsum("ij,jrs->irs", select, new_full, precision=lax.Precision.HIGHEST)

time: 373 us -> 337 us (0.903)
  the two profiles are of different devices: /device:TPU:16 before, /device:TPU:1 now
where the time goes in v1:
time: 337 us
  waiting for transfers between devices  288 us (85%)
  matrix products  15.7 us (5%)
  between operations  14.8 us (4%)
  local copies, waits for them, and re-layouts  13.4 us (4%)
  other arithmetic  3.99 us (1%)
    reduce_scatter x1, waiting for transfers between devices, per_device(): lax.psum_scatter(partial_value, 'dp', scatter_dimension=0, tiled=True)  158 us
    all_gather x1, waiting for transfers between devices, per_device(): grad_full = lax.all_gather(grad_b, 'dp', axis=0, tiled=True)  88 us
    all_gather x1, waiting for transfers between devices, per_device(): all_gather(inner_x, 'stat').sum(axis=0)  42.5 us
    gather x18, local copies, waits for them, and re-layouts  11.7 us
    dot_general x1, matrix products, per_device(): lax.dot_general(activations, out_grads, (((0,), (0,)), ((), ())), preferr...  10.1 us
  transfers between devices with their start and end apart: 3, of which 3 were waited for; matrix products, arithmetic and copies ran while one was open for 0% of the time, Pallas kernels for 0%

profile of v1, /device:TPU:1, one launch (start us, length us, event | category | flops | bytes accessed | tf_op | source)
XLA Modules:
  0.0 336.5 jit_solution(13254435467371964618)
XLA Ops:
  7.2 0.9 copy-done
  8.1 10.1 %fusion.82 = f32[8192,128]{1,0:T(8,128)} fusion(bf16[1024,8192]{1,0:T(8,128)(2,1)} %param.5, bf16[1024,128]{1,0:T(8,128)(2,1)S(1)} %copy-done), kind=kOutput, calls=%fused_computation.101 | convolution fusion | flops 2147483648 | bytes 21233664 | tf_op jit(solution)/shard_map/dot_general | solution.py:40
  18.3 157.9 %reduce-scatter.2.cloned.1.call-done = f32[128,128]{1,0:T(8,128)} async-done(((f32[8192,128]{1,0:T(8,128)}), f32[128,128]{1,0:T(8,128)}) %reduce-scatter.2.cloned.1.call-update) | async-done | bytes 65552 | tf_op jit(solution)/shard_map/reduce_scatter | solution.py:43
  176.2 1.5 convert_element_type.5
  178.1 88.0 %all-gather.4.cloned.1.call-done = bf16[8192,128]{1,0:T(8,128)(2,1)} async-done(((bf16[128,128]{1,0:T(8,128)(2,1)}), bf16[8192,128]{1,0:T(8,128)(2,1)}) %all-gather.4.cloned.1.call-update) | async-done | bytes 2097168 | tf_op jit(solution)/shard_map/all_gather | solution.py:45
  266.1 5.7 %while.2 = (s32[]{:T(128)}, bf16[8192,128]{1,0:T(8,128)(2,1)}, s32[3,2]{0,1:T(2,128)S(1)}, bf16[3,128,128]{2,1,0:T(8,128)(2,1)S(1)}, s32[]{:T(128)}) while((s32[]{:T(128)}, bf16[8192,128]{1,0:T(8,128)(2,1)}, s32[3,2]{0,1:T(2,128)S(1)}, bf16[3,128,128]{2,1,0:T(8,128)(2,1)S(1)}, s32[]{:T(128)}) %tuple.34), condition=%wide.while_cond, body=%wide.while_body.sunk | while | flops 2 | bytes 65641 | solution.py:58
  266.2 0.5 slice.34
  266.7 1.3 bitcast_dynamic-update-slice_fusion.4
  268.1 0.5 slice.34
  268.6 1.3 bitcast_dynamic-update-slice_fusion.4
  270.0 0.5 slice.34
  270.5 1.3 bitcast_dynamic-update-slice_fusion.4
  271.9 6.1 %while.3 = (s32[]{:T(128)}, bf16[8192,128]{1,0:T(8,128)(2,1)}, s32[3,2]{0,1:T(2,128)S(1)}, bf16[3,128,128]{2,1,0:T(8,128)(2,1)S(1)}, s32[]{:T(128)}) while((s32[]{:T(128)}, bf16[8192,128]{1,0:T(8,128)(2,1)}, s32[3,2]{0,1:T(2,128)S(1)}, bf16[3,128,128]{2,1,0:T(8,128)(2,1)S(1)}, s32[]{:T(128)}) %tuple.46), condition=%wide.while_cond.1, body=%wide.while_body.1.sunk | while | flops 2 | bytes 65641 | solution.py:58
  272.0 0.5 slice.35
  272.5 1.4 bitcast_dynamic-update-slice_fusion.5
  274.0 0.5 slice.35
  274.5 1.4 bitcast_dynamic-update-slice_fusion.5
  276.1 0.5 slice.35
  276.6 1.4 bitcast_dynamic-update-slice_fusion.5
  278.0 0.9 fusion.83
  278.9 42.5 %all-gather.6.cloned.1.call-done = f32[24,128,128]{2,1,0:T(8,128)} async-done(((f32[3,128,128]{2,1,0:T(8,128)}), f32[24,128,128]{2,1,0:T(8,128)}) %all-gather.6.cloned.1.call-update) | async-done | bytes 1572880 | tf_op jit(solution)/shard_map/all_gather | solution.py:67
  321.4 1.5 reduce_sum.48
  323.0 0.5 fusion.1
  323.5 0.6 multiply_reduce_fusion
  325.1 0.2 fusion.9
  325.7 0.2 fusion.23
  325.9 0.2 fusion.25
  326.6 0.2 fusion.19
  326.8 0.2 fusion.21
  327.6 0.2 fusion.17
  328.6 0.8 fusion.90
  329.4 0.6 constant_dynamic-slice_fusion.2
  (44 shorter events, 3.4 us)
Async XLA Ops:
  7.2 1.0 copy-start
  7.2 169.0 %reduce-scatter.2.cloned.1.call-start = ((), (), s32[]{:S(2)}) async-start(), calls=%async_computation.1 | async-start | bytes 4259840 | tf_op jit(solution)/shard_map/reduce_scatter | solution.py:43
  18.2 159.5 %copy-start.3 = (s32[192]{0:T(256)S(1)}, s32[192]{0:T(256)}, u32[]{:S(2)}) copy-start(s32[192]{0:T(256)} %param.9) | copy-start | bytes 2308
  18.2 159.7 %copy-start.4 = (s32[192,2]{0,1:T(2,128)S(1)}, s32[192,2]{0,1:T(2,128)}, u32[]{:S(2)}) copy-start(s32[192,2]{0,1:T(2,128)} %param.8) | copy-start | bytes 4612
  18.2 304.7 %copy-start.2 = (f32[3,128,128]{2,1,0:T(8,128)S(1)}, f32[3,128,128]{2,1,0:T(8,128)}, u32[]{:S(2)}) copy-start(f32[3,128,128]{2,1,0:T(8,128)} %param.7) | copy-start | bytes 589828
  18.2 247.9 %all-gather.4.cloned.1.call-start = ((), (), s32[]{:S(2)}) async-start(), calls=%async_computation.2 | async-start | bytes 2129920 | tf_op jit(solution)/shard_map/all_gather | solution.py:45
  177.6 150.9 %copy-start.1 = (bf16[128,128]{1,0:T(8,128)(2,1)S(1)}, bf16[128,128]{1,0:T(8,128)(2,1)}, u32[]{:S(2)}) copy-start(bf16[128,128]{1,0:T(8,128)(2,1)} %convert_element_type.5) | copy-start | bytes 98308
  177.7 143.8 %all-gather.6.cloned.1.call-start = ((), (), s32[]{:S(2)}) async-start(), calls=%async_computation.3 | async-start | bytes 1769472 | tf_op jit(solution)/shard_map/all_gather | solution.py:67
Sparse Core Ops, SparseCore 0:
  18.4 157.7 reduce-scatter.1
  180.1 85.9 all-gather.3
  279.0 42.3 all-gather.5
